TPU v7x, 32 devices: a whole 2x2x4 slice. The times are simulated.
32 devices in a mesh: groups: 2 (over y), markov: 4 (over z), storage: 2 (over x), sub: 2 (over core).
Axes of the slice: x: 2, y: 2, z: 4, core: 2. Of those that a mesh axis runs over, the one named last changes fastest.
Arguments:
- expected_cot: bfloat16 [8192, 2048], P(('groups', 'markov'), ('storage', 'sub')), parts along dimension 0, may hold values from -192 to 192
- value_next: bfloat16 [8192, 2048], P(('groups', 'markov'), ('storage', 'sub')), parts along dimension 0, may hold values from -0.0024414062 to 0.0024414062
- transition: bfloat16 [8192, 4096], P(('groups', 'storage', 'sub'), 'markov'), parts along dimension 0, may hold values from 6.1035156e-05 to 0.0009765625
- section: int32 [2], P('groups'), parts along dimension 0, may hold values from 0 to 51
Outputs:
- section_adjoint: float32 [8192, 2048], P(('groups', 'markov'), ('storage', 'sub')), parts along dimension 0
- transition_grad: float32 [8192, 4096], P(('groups', 'storage', 'sub'), 'markov'), parts along dimension 0
There are 2 independent parts, one for each index of `groups`. A program takes and returns all parts, laid end to end along the dimension named above; each array names one. Nothing has to cross between parts.
All inputs are finite; a program needn't handle non-finite values.
Results may differ from a plain program's by a relative error of at most 0.0003.
Values may be sent and summed in bfloat16 or wider, within the bound.
A program may use at most 64 MiB of HBM per device.

v0:
```python
import jax
import jax.numpy as jnp
from jax import lax
from jax.sharding import PartitionSpec as P

discount_rate = 0.97


def shards(expected_cot, value_next, transition, section):
    discount_factor = jnp.exp(section[0].astype(jnp.float32) * jnp.log(jnp.float32(discount_rate)))
    cotangent_all = lax.all_gather(expected_cot, "markov", axis=0, tiled=True)
    adjoint_sum = lax.dot_general(
        lax.all_gather(transition, ("storage", "sub"), axis=0, tiled=True),
        cotangent_all,
        (((0,), (0,)), ((), ())),
        preferred_element_type=jnp.float32,
    )
    own_states = lax.all_to_all(
        cotangent_all, ("storage", "sub"), split_axis=0, concat_axis=1, tiled=True
    )
    gathered_values = lax.all_gather(value_next, ("storage", "sub"), axis=1, tiled=True)
    gradient_sum = lax.dot_general(
        own_states, gathered_values, (((1,), (1,)), ((), ())), preferred_element_type=jnp.float32
    )
    return (discount_factor * adjoint_sum, discount_factor * gradient_sum)


def solution(mesh):
    return jax.shard_map(
        shards,
        mesh=mesh,
        in_specs=(
            P(("groups", "markov"), ("storage", "sub")),
            P(("groups", "markov"), ("storage", "sub")),
            P(("groups", "storage", "sub"), "markov"),
            P("groups"),
        ),
        out_specs=(
            P(("groups", "markov"), ("storage", "sub")),
            P(("groups", "storage", "sub"), "markov"),
        ),
        check_vma=False,
    )
```

profile of v0, /device:TPU:1, one launch (start us, length us, event | category | flops | bytes accessed | tf_op | source)
XLA Modules:
  0.0 231.9 jit_solution(16197326605313307399)
XLA Ops:
  7.2 0.0 all-gather.6.cloned.1.call-start
  7.2 0.7 all-gather.6.cloned.1.call-update
  7.9 0.0 all-gather.8.cloned.1.call-start
  7.9 0.7 all-gather.8.cloned.1.call-update
  8.6 0.0 all-gather.4.cloned.1.call-start
  8.7 0.7 all-gather.4.cloned.1.call-update
  9.4 82.9 %all-gather.6.cloned.1.call-done = bf16[4096,512]{1,0:T(8,128)(2,1)} async-done(((bf16[1024,512]{1,0:T(8,128)(2,1)}), bf16[4096,512]{1,0:T(8,128)(2,1)}) %all-gather.6.cloned.1.call-update) | async-done | bytes 4194320 | tf_op jit(solution)/shard_map/all_gather | solution.py:11
  92.2 5.6 %all-to-all-start = ((bf16[4,1024,512]{2,1,0:T(8,128)(2,1)}), bf16[4,1024,512]{2,1,0:T(8,128)(2,1)}, u32[]{:S(2)}, u32[]{:S(2)}) async-start(bf16[4,1024,512]{2,1,0:T(8,128)(2,1)} %bitcast.8), calls=%async_computation | async-start | bytes 8388608 | tf_op jit(solution)/shard_map/all_to_all | solution.py:18
  98.6 73.6 %all-to-all-done = bf16[4,1024,512]{2,1,0:T(8,128)(2,1)} async-done(((bf16[4,1024,512]{2,1,0:T(8,128)(2,1)}), bf16[4,1024,512]{2,1,0:T(8,128)(2,1)}, u32[]{:S(2)}, u32[]{:S(2)}) %all-to-all-start) | async-done | bytes 4194336 | tf_op jit(solution)/shard_map/all_to_all | solution.py:18
  172.2 6.3 %copy.6 = bf16[1024,4,512]{0,2,1:T(8,128)(2,1)} copy(bf16[1024,4,512]{2,0,1:T(8,128)(2,1)} %bitcast.2) | data formatting | bytes 8388608 | tf_op jit(solution)/shard_map/all_to_all | solution.py:18
  178.5 0.0 all-gather.8.cloned.1.call-done
  178.5 10.1 %convolution_multiply_fusion = f32[1024,1024]{1,0:T(8,128)} fusion(bf16[1024,2048]{0,1:T(8,128)(2,1)} %bitcast.9, bf16[1024,2048]{1,0:T(8,128)(2,1)} %all-gather.8.cloned.1.call-done, f32[]{:T(128)} %bitcast), kind=kOutput, calls=%fused_computation | convolution fusion | flops 4296015872 | bytes 12582916 | tf_op jit(solution)/shard_map/dot_general | solution.py:22
  188.6 26.3 %all-gather.4.cloned.1.call-done = bf16[4096,1024]{1,0:T(8,128)(2,1)} async-done(((bf16[1024,1024]{1,0:T(8,128)(2,1)}), bf16[4096,1024]{1,0:T(8,128)(2,1)}) %all-gather.4.cloned.1.call-update) | async-done | bytes 8388624 | tf_op jit(solution)/shard_map/all_gather | solution.py:13
  214.9 10.4 %convolution_multiply_fusion.1 = f32[1024,512]{1,0:T(8,128)} fusion(bf16[4096,1024]{1,0:T(8,128)(2,1)} %all-gather.4.cloned.1.call-done, bf16[4096,512]{1,0:T(8,128)(2,1)} %all-gather.6.cloned.1.call-done, f32[]{:T(128)} %bitcast), kind=kOutput, calls=%fused_computation.1 | convolution fusion | flops 4295491584 | bytes 14680068 | tf_op jit(solution)/shard_map/dot_general | solution.py:12
Async XLA Ops:
  7.2 85.1 %all-gather.6.cloned.1.call-start = ((), (), s32[]{:S(2)}) async-start(), calls=%async_computation.2 | async-start | bytes 5242880 | tf_op jit(solution)/shard_map/all_gather | solution.py:11
  7.9 170.6 %all-gather.8.cloned.1.call-start = ((), (), s32[]{:S(2)}) async-start(), calls=%async_computation.3 | async-start | bytes 5242880 | tf_op jit(solution)/shard_map/all_gather | solution.py:21
  8.6 206.3 %all-gather.4.cloned.1.call-start = ((), (), s32[]{:S(2)}) async-start(), calls=%async_computation.1 | async-start | bytes 10485760 | tf_op jit(solution)/shard_map/all_gather | solution.py:13
  92.2 79.9 %all-to-all-start = ((bf16[4,1024,512]{2,1,0:T(8,128)(2,1)}), bf16[4,1024,512]{2,1,0:T(8,128)(2,1)}, u32[]{:S(2)}, u32[]{:S(2)}) async-start(bf16[4,1024,512]{2,1,0:T(8,128)(2,1)} %bitcast.8), calls=%async_computation | async-start | bytes 8388608 | tf_op jit(solution)/shard_map/all_to_all | solution.py:18
Sparse Core Ops, SparseCore 0:
  9.5 82.6 all-gather.5
  93.8 56.0 all-gather.7
  151.5 63.4 all-gather.3
where the time goes:
time: 232 us
  waiting for transfers between devices  185 us (80%)
  matrix products  20.5 us (9%)
  between operations  14.4 us (6%)
  local copies, waits for them, and re-layouts  6.34 us (3%)
  starting transfers between devices  5.73 us (2%)
    all_gather x1, waiting for transfers between devices, shards(): cotangent_all = lax.all_gather(expected_cot, 'markov', axis=0, tiled=True)  82.9 us
    all_to_all x1, waiting for transfers between devices, shards(): lax.all_to_all(cotangent_all, ('storage', 'sub'), split_axis=0, concat_ax...  73.6 us
    all_gather x1, waiting for transfers between devices, shards(): lax.all_gather(transition, ('storage', 'sub'), axis=0, tiled=True)  26.3 us
    dot_general x1, matrix products, shards(): lax.dot_general(lax.all_gather(transition, ('storage', 'sub'), axis=0, ti...  10.4 us
    dot_general x1, matrix products, shards(): lax.dot_general(own_states, gathered_values, (((1,), (1,)), ((), ())), pr...  10.1 us
    all_to_all x1, local copies, waits for them, and re-layouts, shards(): lax.all_to_all(cotangent_all, ('storage', 'sub'), split_axis=0, concat_ax...  6.34 us
    all_to_all x1, starting transfers between devices, shards(): lax.all_to_all(cotangent_all, ('storage', 'sub'), split_axis=0, concat_ax...  5.62 us
  transfers between devices with their start and end apart: 4, of which 3 were waited for; matrix products, arithmetic and copies ran while one was open for 7% of the time, Pallas kernels for 0%

commit v1 on v0

--- a/solution.py
+++ b/solution.py
@@ -1,13 +1,24 @@
+import functools
+
 import jax
 import jax.numpy as jnp
 from jax import lax
+from jax.experimental import pallas as pl
+from jax.experimental.pallas import tpu as pltpu
 from jax.sharding import PartitionSpec as P
 
 discount_rate = 0.97
-
-
-def shards(expected_cot, value_next, transition, section):
-    discount_factor = jnp.exp(section[0].astype(jnp.float32) * jnp.log(jnp.float32(discount_rate)))
+MESH = pl.DeviceIdType.MESH
+PIECES = 2
+TILE = 256
+
+
+def discount_of(section):
+    return jnp.exp(section[0].astype(jnp.float32) * jnp.log(jnp.float32(discount_rate)))
+
+
+def gathered(expected_cot, value_next, transition, section):
+    discount_factor = discount_of(section)
     cotangent_all = lax.all_gather(expected_cot, "markov", axis=0, tiled=True)
     adjoint_sum = lax.dot_general(
         lax.all_gather(transition, ("storage", "sub"), axis=0, tiled=True),
@@ -25,9 +36,298 @@
     return (discount_factor * adjoint_sum, discount_factor * gradient_sum)
 
 
+def kernel(
+    n_z, c_in, v_in, t_in, adj, grad, c_all, c_row, t_all, v_all,
+    local_sem, z_recv, up_send, down_send, tx_send, tx_recv, vx_send, vx_recv,
+    tf_send, tf_recv, vf_send, vf_recv, tp_send, tp_recv, vp_send, vp_recv,
+    cp_send, cp_recv, row_send, row_recv, flow_send,
+):
+    g, m = lax.axis_index("groups"), lax.axis_index("markov")
+    s, u = lax.axis_index("storage"), lax.axis_index("sub")
+    far = 1 - s
+    j, p = 2 * s + u, 2 * s + 1 - u
+    o, q = 2 * far + u, 2 * far + 1 - u
+    partner, across, crossed = (g, m, s, 1 - u), (g, m, far, u), (g, m, far, 1 - u)
+    above, below = (g, lax.rem(m + 1, n_z), s, u), (g, lax.rem(m + n_z - 1, n_z), s, u)
+    has_up, has_down = m < n_z - 1, m > 0
+
+    def crossing_row(chip, z):
+        return jnp.clip(z, 2 * chip, 2 * chip + 1)
+
+    sent_row = crossing_row(far, m)
+    sent_own = sent_row == m
+    by_x = crossing_row(s, m) == j
+    flow_up = (m >= j) & has_up & (crossing_row(s, m + 1) != j)
+    flow_down = (m <= j) & has_down & (crossing_row(s, m - 1) != j)
+
+    def rows(ref, piece, *lead):
+        step = ref.shape[-2] // PIECES
+        return ref.at[(*lead, pl.ds(piece * step, step))]
+
+    def remote(src, dst, send, recv, to):
+        return pltpu.make_async_remote_copy(
+            src_ref=src, dst_ref=dst, send_sem=send, recv_sem=recv, device_id=to, device_id_type=MESH
+        )
+
+    def z_up(r, c, src=None):
+        dst = rows(c_all, c, r)
+        return remote(dst if src is None else src, dst, up_send.at[r, c], z_recv.at[r, c], above)
+
+    def z_down(r, c, src=None):
+        dst = rows(c_all, c, r)
+        return remote(dst if src is None else src, dst, down_send.at[r, c], z_recv.at[r, c], below)
+
+    def to_across(inp, buf, c, send, recv):
+        return remote(rows(inp, c), rows(buf, c, j), send.at[c], recv.at[c], across)
+
+    def to_partner(inp, buf, c, send, recv):
+        return remote(rows(inp, c), rows(buf, c, j), send.at[c], recv.at[c], partner)
+
+    def forward(buf, c, send, recv):
+        part = rows(buf, c, o)
+        return remote(part, part, send.at[c], recv.at[c], partner)
+
+    def row_to(c, core, src):
+        return remote(
+            src, rows(c_row, c, j), row_send.at[c], row_recv.at[u, c], (g, m, far, core)
+        )
+
+    def start_row(c, own):
+        src = rows(c_in, c) if own else rows(c_all, c, sent_row)
+        row_to(c, sent_row - 2 * far, src).start()
+
+    def flow(b, c, to):
+        part = rows(c_row, c, 2 * far + b)
+        return remote(part, part, flow_send.at[b, c], row_recv.at[b, c], to)
+
+    def cells_to_partner(c, src):
+        return remote(src, rows(c_row, c, j), cp_send.at[c], cp_recv.at[c], partner)
+
+    def got(buf, slot, c, recv):
+        part = rows(buf, c, slot)
+        remote(part, part, recv, recv, partner).wait_recv()
+
+    barrier = pltpu.get_barrier_semaphore()
+    for to in (partner, across, crossed):
+        pl.semaphore_signal(barrier, inc=1, device_id=to, device_id_type=MESH)
+
+    @pl.when(has_up)
+    def _():
+        pl.semaphore_signal(barrier, inc=1, device_id=above, device_id_type=MESH)
+
+    @pl.when(has_down)
+    def _():
+        pl.semaphore_signal(barrier, inc=1, device_id=below, device_id_type=MESH)
+
+    owns = (
+        pltpu.make_async_copy(c_in, c_all.at[m], local_sem.at[0]),
+        pltpu.make_async_copy(t_in, t_all.at[j], local_sem.at[1]),
+        pltpu.make_async_copy(v_in, v_all.at[j], local_sem.at[2]),
+    )
+    for copy in owns:
+        copy.start()
+    pl.semaphore_wait(barrier, 3 + has_up.astype(jnp.int32) + has_down.astype(jnp.int32))
+
+    for c in range(PIECES):
+
+        @pl.when(has_up)
+        def _():
+            z_up(m, c, rows(c_in, c)).start()
+
+        @pl.when(has_down)
+        def _():
+            z_down(m, c, rows(c_in, c)).start()
+
+        @pl.when(sent_own)
+        def _():
+            start_row(c, True)
+
+    for c in range(PIECES):
+        to_across(t_in, t_all, c, tx_send, tx_recv).start()
+    for c in range(PIECES):
+        to_across(v_in, v_all, c, vx_send, vx_recv).start()
+    for c in range(PIECES):
+        to_partner(t_in, t_all, c, tp_send, tp_recv).start()
+        to_partner(v_in, v_all, c, vp_send, vp_recv).start()
+
+        @pl.when(m == p)
+        def _():
+            cells_to_partner(c, rows(c_in, c)).start()
+
+    adj[...] = jnp.zeros_like(adj)
+    grad[...] = jnp.zeros_like(grad)
+    for copy in owns:
+        copy.wait()
+
+    def add_adj(k):
+        @pl.loop(0, adj.shape[0] // TILE)
+        def _(i):
+            at = pl.ds(pl.multiple_of(i * TILE, TILE), TILE)
+            adj[at, :] += lax.dot_general(
+                t_all[k, :, at], c_all[k], (((0,), (0,)), ((), ())),
+                preferred_element_type=jnp.float32,
+            )
+
+    def add_grad(buf, k_rows, k):
+        @pl.loop(0, grad.shape[0] // TILE)
+        def _(i):
+            at = pl.ds(pl.multiple_of(i * TILE, TILE), TILE)
+            grad[at, :] += lax.dot_general(
+                buf[k_rows, at, :], v_all[k], (((1,), (1,)), ((), ())),
+                preferred_element_type=jnp.float32,
+            )
+
+    def arrived(r, c):
+        @pl.when(r == p)
+        def _():
+            cells_to_partner(c, rows(c_all, c, r)).start()
+
+        @pl.when((r == sent_row) & jnp.logical_not(sent_own))
+        def _():
+            start_row(c, False)
+
+    def z_step(d):
+        for c in range(PIECES):
+
+            @pl.when(m - d >= 0)
+            def _():
+                r = m - d
+                got(c_all, r, c, z_recv.at[r, c])
+
+                @pl.when(has_up)
+                def _():
+                    z_up(r, c).start()
+
+                arrived(r, c)
+
+            @pl.when(m + d <= n_z - 1)
+            def _():
+                r = m + d
+                got(c_all, r, c, z_recv.at[r, c])
+
+                @pl.when(has_down)
+                def _():
+                    z_down(r, c).start()
+
+                arrived(r, c)
+
+    def row_step(when):
+        @pl.when(when)
+        def _():
+            for c in range(PIECES):
+                for b in range(2):
+                    got(c_row, 2 * far + b, c, row_recv.at[b, c])
+
+                    @pl.when(flow_up)
+                    def _():
+                        flow(b, c, above).start()
+
+                    @pl.when(flow_down)
+                    def _():
+                        flow(b, c, below).start()
+
+    away = jnp.abs(m - j)
+
+    def relay(buf, c, send, recv, x_recv):
+        got(buf, o, c, x_recv.at[c])
+        forward(buf, c, send, recv).start()
+
+    z_step(1)
+    row_step(away == 0)
+    relay(t_all, 0, tf_send, tf_recv, tx_recv)
+    z_step(2)
+    row_step(jnp.logical_not(by_x) & (away == 1))
+    relay(t_all, 1, tf_send, tf_recv, tx_recv)
+    z_step(3)
+    row_step(jnp.logical_not(by_x) & (away == 2))
+    for c in range(PIECES):
+        got(t_all, p, c, tp_recv.at[c])
+    add_adj(j)
+    add_adj(p)
+    relay(v_all, 0, vf_send, vf_recv, vx_recv)
+    for c in range(PIECES):
+        got(v_all, p, c, vp_recv.at[c])
+        got(c_row, p, c, cp_recv.at[c])
+    add_grad(c_all, j, j)
+    add_grad(c_row, p, p)
+    relay(v_all, 1, vf_send, vf_recv, vx_recv)
+    add_adj(o)
+    for c in range(PIECES):
+        got(t_all, q, c, tf_recv.at[c])
+    add_adj(q)
+    row_step((by_x & (away > 0)) | (jnp.logical_not(by_x) & (away == 3)))
+    add_grad(c_row, o, o)
+    for c in range(PIECES):
+        got(v_all, q, c, vf_recv.at[c])
+    add_grad(c_row, q, q)
+
+    for c in range(PIECES):
+        for r in range(n_z):
+
+            @pl.when(has_up & (r <= m))
+            def _():
+                z_up(r, c).wait_send()
+
+            @pl.when(has_down & (r >= m))
+            def _():
+                z_down(r, c).wait_send()
+
+        row_to(c, u, rows(c_in, c)).wait_send()
+        cells_to_partner(c, rows(c_in, c)).wait_send()
+        to_across(t_in, t_all, c, tx_send, tx_recv).wait_send()
+        to_across(v_in, v_all, c, vx_send, vx_recv).wait_send()
+        to_partner(t_in, t_all, c, tp_send, tp_recv).wait_send()
+        to_partner(v_in, v_all, c, vp_send, vp_recv).wait_send()
+        forward(t_all, c, tf_send, tf_recv).wait_send()
+        forward(v_all, c, vf_send, vf_recv).wait_send()
+        for b in range(2):
+
+            @pl.when(flow_up | flow_down)
+            def _():
+                flow(b, c, above).wait_send()
+
+
+def exchanged(n_z, expected_cot, value_next, transition, section):
+    states, cells = expected_cot.shape
+    current, following = transition.shape
+    dma = pltpu.SemaphoreType.DMA
+    piece = dma((PIECES,))
+    adjoint_sum, gradient_sum = pl.pallas_call(
+        functools.partial(kernel, n_z),
+        out_shape=(
+            jax.ShapeDtypeStruct((following, cells), jnp.float32),
+            jax.ShapeDtypeStruct((current, following), jnp.float32),
+        ),
+        in_specs=[pl.BlockSpec(memory_space=pl.ANY)] * 3,
+        out_specs=(pl.BlockSpec(memory_space=pltpu.VMEM),) * 2,
+        scratch_shapes=[
+            pltpu.VMEM((n_z, states, cells), jnp.bfloat16),
+            pltpu.VMEM((4, current, cells), jnp.bfloat16),
+            pltpu.VMEM((4, current, following), jnp.bfloat16),
+            pltpu.VMEM((4, states, cells), jnp.bfloat16),
+            dma((3,)),
+            dma((n_z, PIECES)),
+            dma((n_z, PIECES)),
+            dma((n_z, PIECES)),
+            *([piece] * 14),
+            piece,
+            dma((2, PIECES)),
+            dma((2, PIECES)),
+        ],
+        compiler_params=pltpu.CompilerParams(
+            collective_id=0, has_side_effects=True, vmem_limit_bytes=48 * 1024 * 1024
+        ),
+    )(expected_cot, value_next, transition)
+    discount_factor = discount_of(section)
+    return (discount_factor * adjoint_sum, discount_factor * gradient_sum)
+
+
 def solution(mesh):
+    shape = mesh.shape
+    paired = shape["storage"] == 2 and shape["sub"] == 2 and shape["markov"] == 4
+    body = functools.partial(exchanged, shape["markov"]) if paired else gathered
     return jax.shard_map(
-        shards,
+        body,
         mesh=mesh,
         in_specs=(
             P(("groups", "markov"), ("storage", "sub")),

time: 232 us -> 122 us (0.53)
  waiting for transfers between devices: 185 us -> 0 us
  Pallas kernels: 0 us -> 113 us
  matrix products: 20.5 us -> 0 us
  between operations: 14.4 us -> 1.35 us
  starting transfers between devices: 5.73 us -> 0 us
  other arithmetic: 0 us -> 3.99 us
  local copies, waits for them, and re-layouts: 6.34 us -> 3.84 us
    pallas_call x0 -> x1, Pallas kernels: none -> 113 us  [exchanged(): pl.pallas_call(functools.partial(kernel, n_z), out_shape=(jax.ShapeDtypeS...]
    all_gather x3 -> x0, waiting for transfers between devices: 109 us -> none  [the longest x1 82.9 us: shards(): cotangent_all = lax.all_gather(expected_cot, 'markov', axis=0, tiled=True)]
    all_to_all x1 -> x0, waiting for transfers between devices: 73.6 us -> none  [shards(): lax.all_to_all(cotangent_all, ('storage', 'sub'), split_axis=0, concat_ax...]
    dot_general x2 -> x0, matrix products: 20.5 us -> none  [the longest x1 10.4 us: shards(): lax.dot_general(lax.all_gather(transition, ('storage', 'sub'), axis=0, ti...]
    all_to_all x1 -> x0, local copies, waits for them, and re-layouts: 6.34 us -> none  [shards(): lax.all_to_all(cotangent_all, ('storage', 'sub'), split_axis=0, concat_ax...]
    all_to_all x1 -> x0, starting transfers between devices: 5.62 us -> none  [shards(): lax.all_to_all(cotangent_all, ('storage', 'sub'), split_axis=0, concat_ax...]
    mul x0 -> x2, other arithmetic: none -> 3.99 us  [exchanged(): return (discount_factor * adjoint_sum, discount_factor * gradient_sum)]
    unnamed x0 -> x6, local copies, waits for them, and re-layouts: none -> 3.84 us
  transfers between devices with their start and end apart: 4 -> 0, of which waited for: 3 -> 0; matrix products, arithmetic and copies ran while one was open for 7% -> 0% of each run, Pallas kernels for 0% -> 0%
where the time goes in v1:
time: 122 us
  Pallas kernels  113 us (93%)
  other arithmetic  3.99 us (3%)
  local copies, waits for them, and re-layouts  3.84 us (3%)
  between operations  1.35 us (1%)
    pallas_call x1, Pallas kernels, exchanged(): pl.pallas_call(functools.partial(kernel, n_z), out_shape=(jax.ShapeDtypeS...  113 us
    mul x2, other arithmetic, exchanged(): return (discount_factor * adjoint_sum, discount_factor * gradient_sum)  3.99 us
    unnamed x6, local copies, waits for them, and re-layouts  3.84 us

profile of v1, /device:TPU:1, one launch (start us, length us, event | category | flops | bytes accessed | tf_op | source)
XLA Modules:
  0.0 121.8 jit_solution(13284900727790642116)
XLA Ops:
  1.3 0.0 copy-start
  1.3 1.2 copy-done
  2.5 0.0 copy-start.1
  2.5 1.2 %copy-done.1 = bf16[1024,512]{1,0:T(8,128)(2,1)S(1)} copy-done((bf16[1024,512]{1,0:T(8,128)(2,1)S(1)}, bf16[1024,512]{1,0:T(8,128)(2,1)}, u32[]{:S(2)}) %copy-start.1) | copy-done | bytes 1048600
  3.8 112.6 %shard_map.59 = (f32[1024,512]{1,0:T(8,128)S(1)}, f32[1024,1024]{1,0:T(8,128)}) custom-call(bf16[1024,512]{1,0:T(8,128)(2,1)S(1)} %copy-done, bf16[1024,512]{1,0:T(8,128)(2,1)S(1)} %copy-done.1, bf16[1024,1024]{1,0:T(8,128)(2,1)} %t_in.1), custom_call_target="tpu_custom_call" | custom-call | tf_op jit(solution)/shard_map/pallas_call | solution.py:295
  116.4 0.0 copy-start.2
  116.4 1.5 %broadcast_multiply_fusion.1 = f32[1024,512]{1,0:T(8,128)} fusion(f32[1024,512]{1,0:T(8,128)S(1)} %get-tuple-element.4, f32[]{:T(128)} %bitcast), kind=kLoop, calls=%fused_computation.1 | loop fusion | flops 524288 | bytes 4194308 | tf_op jit(solution)/shard_map/mul | solution.py:322
  118.0 1.4 %copy-done.2 = f32[1024,1024]{1,0:T(8,128)S(1)} copy-done((f32[1024,1024]{1,0:T(8,128)S(1)}, f32[1024,1024]{1,0:T(8,128)}, u32[]{:S(2)}) %copy-start.2) | copy-done | bytes 4194328
  119.3 2.4 %broadcast_multiply_fusion = f32[1024,1024]{1,0:T(8,128)} fusion(f32[1024,1024]{1,0:T(8,128)S(1)} %copy-done.2, f32[]{:T(128)} %bitcast), kind=kLoop, calls=%fused_computation | loop fusion | flops 1048576 | bytes 8388612 | tf_op jit(solution)/shard_map/mul | solution.py:322
Async XLA Ops:
  1.3 1.2 %copy-start = (bf16[1024,512]{1,0:T(8,128)(2,1)S(1)}, bf16[1024,512]{1,0:T(8,128)(2,1)}, u32[]{:S(2)}) copy-start(bf16[1024,512]{1,0:T(8,128)(2,1)} %c_in.1) | copy-start | bytes 3145732
  2.5 1.2 %copy-start.1 = (bf16[1024,512]{1,0:T(8,128)(2,1)S(1)}, bf16[1024,512]{1,0:T(8,128)(2,1)}, u32[]{:S(2)}) copy-start(bf16[1024,512]{1,0:T(8,128)(2,1)} %v_in.1) | copy-start | bytes 3145732
  116.4 2.9 %copy-start.2 = (f32[1024,1024]{1,0:T(8,128)S(1)}, f32[1024,1024]{1,0:T(8,128)}, u32[]{:S(2)}) copy-start(f32[1024,1024]{1,0:T(8,128)} %get-tuple-element.5) | copy-start | bytes 12582916

commit v2 on v1

--- a/solution.py
+++ b/solution.py
@@ -11,6 +11,7 @@
 MESH = pl.DeviceIdType.MESH
 PIECES = 2
 TILE = 256
+VMEM_BYTES = 34 * 1024 * 1024
 
 
 def discount_of(section):
@@ -156,8 +157,6 @@
 
     adj[...] = jnp.zeros_like(adj)
     grad[...] = jnp.zeros_like(grad)
-    for copy in owns:
-        copy.wait()
 
     def add_adj(k):
         @pl.loop(0, adj.shape[0] // TILE)
@@ -168,12 +167,12 @@
                 preferred_element_type=jnp.float32,
             )
 
-    def add_grad(buf, k_rows, k):
-        @pl.loop(0, grad.shape[0] // TILE)
+    def add_grad(buf, k, top=0, many=grad.shape[0], cut=pl.ds(0, grad.shape[1])):
+        @pl.loop(0, many // TILE)
         def _(i):
-            at = pl.ds(pl.multiple_of(i * TILE, TILE), TILE)
-            grad[at, :] += lax.dot_general(
-                buf[k_rows, at, :], v_all[k], (((1,), (1,)), ((), ())),
+            at = pl.ds(pl.multiple_of(top + i * TILE, TILE), TILE)
+            grad[at, cut] += lax.dot_general(
+                buf[k, at, :], v_all[k, cut, :], (((1,), (1,)), ((), ())),
                 preferred_element_type=jnp.float32,
             )
 
@@ -186,80 +185,132 @@
         def _():
             start_row(c, False)
 
-    def z_step(d):
-        for c in range(PIECES):
-
-            @pl.when(m - d >= 0)
-            def _():
-                r = m - d
-                got(c_all, r, c, z_recv.at[r, c])
-
-                @pl.when(has_up)
+    def z_step(d, c):
+        @pl.when(m - d >= 0)
+        def _():
+            r = m - d
+            got(c_all, r, c, z_recv.at[r, c])
+
+            @pl.when(has_up)
+            def _():
+                z_up(r, c).start()
+
+            arrived(r, c)
+
+        @pl.when(m + d <= n_z - 1)
+        def _():
+            r = m + d
+            got(c_all, r, c, z_recv.at[r, c])
+
+            @pl.when(has_down)
+            def _():
+                z_down(r, c).start()
+
+            arrived(r, c)
+
+    def row_step(c, when):
+        @pl.when(when)
+        def _():
+            for b in range(2):
+                got(c_row, 2 * far + b, c, row_recv.at[b, c])
+
+                @pl.when(flow_up)
                 def _():
-                    z_up(r, c).start()
-
-                arrived(r, c)
-
-            @pl.when(m + d <= n_z - 1)
-            def _():
-                r = m + d
-                got(c_all, r, c, z_recv.at[r, c])
-
-                @pl.when(has_down)
+                    flow(b, c, above).start()
+
+                @pl.when(flow_down)
                 def _():
-                    z_down(r, c).start()
-
-                arrived(r, c)
-
-    def row_step(when):
-        @pl.when(when)
-        def _():
-            for c in range(PIECES):
-                for b in range(2):
-                    got(c_row, 2 * far + b, c, row_recv.at[b, c])
-
-                    @pl.when(flow_up)
-                    def _():
-                        flow(b, c, above).start()
-
-                    @pl.when(flow_down)
-                    def _():
-                        flow(b, c, below).start()
-
-    away = jnp.abs(m - j)
+                    flow(b, c, below).start()
+
+    away, away_p = jnp.abs(m - j), jnp.abs(m - p)
+    row_first = crossing_row(s, m) == m
 
     def relay(buf, c, send, recv, x_recv):
         got(buf, o, c, x_recv.at[c])
         forward(buf, c, send, recv).start()
 
-    z_step(1)
-    row_step(away == 0)
-    relay(t_all, 0, tf_send, tf_recv, tx_recv)
-    z_step(2)
-    row_step(jnp.logical_not(by_x) & (away == 1))
-    relay(t_all, 1, tf_send, tf_recv, tx_recv)
-    z_step(3)
-    row_step(jnp.logical_not(by_x) & (away == 2))
-    for c in range(PIECES):
-        got(t_all, p, c, tp_recv.at[c])
-    add_adj(j)
-    add_adj(p)
-    relay(v_all, 0, vf_send, vf_recv, vx_recv)
-    for c in range(PIECES):
-        got(v_all, p, c, vp_recv.at[c])
-        got(c_row, p, c, cp_recv.at[c])
-    add_grad(c_all, j, j)
-    add_grad(c_row, p, p)
-    relay(v_all, 1, vf_send, vf_recv, vx_recv)
-    add_adj(o)
-    for c in range(PIECES):
-        got(t_all, q, c, tf_recv.at[c])
-    add_adj(q)
-    row_step((by_x & (away > 0)) | (jnp.logical_not(by_x) & (away == 3)))
-    add_grad(c_row, o, o)
-    for c in range(PIECES):
-        got(v_all, q, c, vf_recv.at[c])
-    add_grad(c_row, q, q)
+    def partner_blocks():
+        for c in range(PIECES):
+            got(t_all, p, c, tp_recv.at[c])
+            got(v_all, p, c, vp_recv.at[c])
+
+    def near(d):
+        @pl.when(away == d)
+        def _():
+            add_adj(j)
+            add_grad(c_all, j)
+
+        @pl.when(away_p == d)
+        def _():
+            add_adj(p)
+
+    def partner_cells():
+        for c in range(PIECES):
+            got(c_row, p, c, cp_recv.at[c])
+        add_grad(c_row, p)
+
+    def far_adj():
+        add_adj(o)
+        for c in range(PIECES):
+            got(t_all, q, c, tf_recv.at[c])
+        add_adj(q)
+
+    def cut_of(c):
+        wide = grad.shape[1] // PIECES
+        return pl.ds(c * wide, wide)
+
+    def grad_by_values(c):
+        @pl.when(row_first)
+        def _():
+            relay(v_all, c, vf_send, vf_recv, vx_recv)
+            add_grad(c_row, o, cut=cut_of(c))
+            got(v_all, q, c, vf_recv.at[c])
+            add_grad(c_row, q, cut=cut_of(c))
+
+    def values_early(c):
+        @pl.when(jnp.logical_not(row_first))
+        def _():
+            relay(v_all, c, vf_send, vf_recv, vx_recv)
+            got(v_all, q, c, vf_recv.at[c])
+
+    def grad_by_rows(c):
+        tall = grad.shape[0] // PIECES
+
+        @pl.when(jnp.logical_not(row_first))
+        def _():
+            add_grad(c_row, o, c * tall, tall)
+            add_grad(c_row, q, c * tall, tall)
+
+    tasks = []
+    block = 22.0
+    for c in range(PIECES):
+        part = block * (c + 1) / PIECES
+        for d in range(1, n_z):
+            tasks.append((block * (d - 1) + part, functools.partial(z_step, d, c)))
+        tasks.append((part + 0.1, functools.partial(row_step, c, away == 0)))
+        for h in range(1, n_z):
+            when = jnp.logical_not(by_x) & (away == h)
+            tasks.append((block * h + part + 0.2, functools.partial(row_step, c, when)))
+        late = by_x & (away > 0)
+        tasks.append((3 * block + part + 0.3, functools.partial(row_step, c, late)))
+        tasks.append(
+            (
+                block + 2 * part,
+                functools.partial(relay, t_all, c, tf_send, tf_recv, tx_recv),
+            )
+        )
+        tasks.append((2 * block + part + 4, functools.partial(values_early, c)))
+        tasks.append((3 * block + part + 1, functools.partial(grad_by_values, c)))
+        tasks.append((3 * block + part + 1.1, functools.partial(grad_by_rows, c)))
+    tasks.append((5.0, partner_blocks))
+    for d in range(n_z):
+        tasks.append((block * d + 0.5 + 5.0 * (d == 0), functools.partial(near, d)))
+    tasks.append((3 * block + 0.7, partner_cells))
+    tasks.append((3 * block + 3, far_adj))
+    for copy in owns:
+        copy.wait()
+    for _, task in sorted(tasks, key=lambda entry: entry[0]):
+        task()
 
     for c in range(PIECES):
         for r in range(n_z):
@@ -298,7 +349,7 @@
             jax.ShapeDtypeStruct((following, cells), jnp.float32),
             jax.ShapeDtypeStruct((current, following), jnp.float32),
         ),
-        in_specs=[pl.BlockSpec(memory_space=pl.ANY)] * 3,
+        in_specs=[pl.BlockSpec(memory_space=pltpu.HBM)] * 3,
         out_specs=(pl.BlockSpec(memory_space=pltpu.VMEM),) * 2,
         scratch_shapes=[
             pltpu.VMEM((n_z, states, cells), jnp.bfloat16),
@@ -315,7 +366,7 @@
             dma((2, PIECES)),
         ],
         compiler_params=pltpu.CompilerParams(
-            collective_id=0, has_side_effects=True, vmem_limit_bytes=48 * 1024 * 1024
+            collective_id=0, has_side_effects=True, vmem_limit_bytes=VMEM_BYTES
         ),
     )(expected_cot, value_next, transition)
     discount_factor = discount_of(section)

time: 122 us -> 117 us (0.959)
  Pallas kernels: 113 us -> 107 us
    pallas_call x1, Pallas kernels: 113 us -> 107 us  [exchanged(): pl.pallas_call(functools.partial(kernel, n_z), out_shape=(jax.ShapeDtypeS...]
where the time goes in v2:
time: 117 us
  Pallas kernels  107 us (91%)
  other arithmetic  4.39 us (4%)
  local copies, waits for them, and re-layouts  4.03 us (3%)
  between operations  1.34 us (1%)
    pallas_call x1, Pallas kernels, exchanged(): pl.pallas_call(functools.partial(kernel, n_z), out_shape=(jax.ShapeDtypeS...  107 us
    mul x2, other arithmetic, exchanged(): return (discount_factor * adjoint_sum, discount_factor * gradient_sum)  4.39 us
    unnamed x6, local copies, waits for them, and re-layouts  4.03 us

profile of v2, /device:TPU:1, one launch (start us, length us, event | category | flops | bytes accessed | tf_op | source)
XLA Modules:
  0.0 117.1 jit_solution(11901787061847372378)
XLA Ops:
  1.3 0.0 copy-start
  1.3 1.6 %copy-done = bf16[1024,1024]{1,0:T(8,128)(2,1)S(1)} copy-done((bf16[1024,1024]{1,0:T(8,128)(2,1)S(1)}, bf16[1024,1024]{1,0:T(8,128)(2,1)}, u32[]{:S(2)}) %copy-start) | copy-done | bytes 2097176
  2.9 0.0 copy-start.1
  2.9 1.2 %copy-done.1 = bf16[1024,512]{1,0:T(8,128)(2,1)S(1)} copy-done((bf16[1024,512]{1,0:T(8,128)(2,1)S(1)}, bf16[1024,512]{1,0:T(8,128)(2,1)}, u32[]{:S(2)}) %copy-start.1) | copy-done | bytes 1048600
  4.1 0.0 copy-start.2
  4.1 1.2 %copy-done.2 = bf16[1024,512]{1,0:T(8,128)(2,1)S(1)} copy-done((bf16[1024,512]{1,0:T(8,128)(2,1)S(1)}, bf16[1024,512]{1,0:T(8,128)(2,1)}, u32[]{:S(2)}) %copy-start.2) | copy-done | bytes 1048600
  5.4 107.3 %shard_map.59 = (f32[1024,512]{1,0:T(8,128)S(1)}, f32[1024,1024]{1,0:T(8,128)S(1)}) custom-call(bf16[1024,512]{1,0:T(8,128)(2,1)S(1)} %copy-done.1, bf16[1024,512]{1,0:T(8,128)(2,1)S(1)} %copy-done.2, bf16[1024,1024]{1,0:T(8,128)(2,1)S(1)} %copy-done), custom_call_target="tpu_custom_call" | custom-call | tf_op jit(solution)/shard_map/pallas_call | solution.py:346
  112.7 1.5 %broadcast_multiply_fusion.1 = f32[1024,512]{1,0:T(8,128)} fusion(f32[1024,512]{1,0:T(8,128)S(1)} %get-tuple-element.4, f32[]{:T(128)} %bitcast), kind=kLoop, calls=%fused_computation.1 | loop fusion | flops 524288 | bytes 4194308 | tf_op jit(solution)/shard_map/mul | solution.py:373
  114.2 2.8 %broadcast_multiply_fusion = f32[1024,1024]{1,0:T(8,128)} fusion(f32[1024,1024]{1,0:T(8,128)S(1)} %get-tuple-element.5, f32[]{:T(128)} %bitcast), kind=kLoop, calls=%fused_computation | loop fusion | flops 1048576 | bytes 8388612 | tf_op jit(solution)/shard_map/mul | solution.py:373
Async XLA Ops:
  1.3 1.6 %copy-start = (bf16[1024,1024]{1,0:T(8,128)(2,1)S(1)}, bf16[1024,1024]{1,0:T(8,128)(2,1)}, u32[]{:S(2)}) copy-start(bf16[1024,1024]{1,0:T(8,128)(2,1)} %t_in.1) | copy-start | bytes 6291460
  2.9 1.2 %copy-start.1 = (bf16[1024,512]{1,0:T(8,128)(2,1)S(1)}, bf16[1024,512]{1,0:T(8,128)(2,1)}, u32[]{:S(2)}) copy-start(bf16[1024,512]{1,0:T(8,128)(2,1)} %c_in.1) | copy-start | bytes 3145732
  4.1 1.2 %copy-start.2 = (bf16[1024,512]{1,0:T(8,128)(2,1)S(1)}, bf16[1024,512]{1,0:T(8,128)(2,1)}, u32[]{:S(2)}) copy-start(bf16[1024,512]{1,0:T(8,128)(2,1)} %v_in.1) | copy-start | bytes 3145732

commit v3 on v2

--- a/solution.py
+++ b/solution.py
@@ -208,22 +208,29 @@
 
             arrived(r, c)
 
+    def flow_on(c, when):
+        @pl.when(when & flow_up)
+        def _():
+            for b in range(2):
+                flow(b, c, above).start()
+
+        @pl.when(when & flow_down)
+        def _():
+            for b in range(2):
+                flow(b, c, below).start()
+
     def row_step(c, when):
         @pl.when(when)
         def _():
             for b in range(2):
                 got(c_row, 2 * far + b, c, row_recv.at[b, c])
 
-                @pl.when(flow_up)
-                def _():
-                    flow(b, c, above).start()
-
-                @pl.when(flow_down)
-                def _():
-                    flow(b, c, below).start()
+            flow_on(c, jnp.logical_not(one_hop))
 
     away, away_p = jnp.abs(m - j), jnp.abs(m - p)
     row_first = crossing_row(s, m) == m
+    one_hop = (j == 1) | (j == 2)
+    rows_late = one_hop & jnp.logical_not(by_x) & (away == 1)
 
     def relay(buf, c, send, recv, x_recv):
         got(buf, o, c, x_recv.at[c])
@@ -263,9 +270,24 @@
         @pl.when(row_first)
         def _():
             relay(v_all, c, vf_send, vf_recv, vx_recv)
-            add_grad(c_row, o, cut=cut_of(c))
-            got(v_all, q, c, vf_recv.at[c])
-            add_grad(c_row, q, cut=cut_of(c))
+
+            @pl.when(jnp.logical_not(rows_late))
+            def _():
+                add_grad(c_row, o, cut=cut_of(c))
+                got(v_all, q, c, vf_recv.at[c])
+                add_grad(c_row, q, cut=cut_of(c))
+
+            @pl.when(rows_late)
+            def _():
+                for b in range(2):
+                    got(c_row, 2 * far + b, c, row_recv.at[b, c])
+                tall = grad.shape[0] // PIECES
+                for k in (o, q):
+                    if c:
+                        add_grad(c_row, k, c * tall, tall, pl.ds(0, cut_of(c).start))
+                    if k is q:
+                        got(v_all, q, c, vf_recv.at[c])
+                    add_grad(c_row, k, 0, (c + 1) * tall, cut_of(c))
 
     def values_early(c):
         @pl.when(jnp.logical_not(row_first))
@@ -289,8 +311,9 @@
             tasks.append((block * (d - 1) + part, functools.partial(z_step, d, c)))
         tasks.append((part + 0.1, functools.partial(row_step, c, away == 0)))
         for h in range(1, n_z):
-            when = jnp.logical_not(by_x) & (away == h)
+            when = jnp.logical_not(by_x | rows_late) & (away == h)
             tasks.append((block * h + part + 0.2, functools.partial(row_step, c, when)))
+        tasks.append((block + part + 0.15, functools.partial(flow_on, c, one_hop & (away == 0))))
         late = by_x & (away > 0)
         tasks.append((3 * block + part + 0.3, functools.partial(row_step, c, late)))
         tasks.append(
@@ -368,7 +391,7 @@
         compiler_params=pltpu.CompilerParams(
             collective_id=0, has_side_effects=True, vmem_limit_bytes=VMEM_BYTES
         ),
-    )(expected_cot, value_next, transition)
+    )(*(pltpu.with_memory_space_constraint(x, pltpu.HBM) for x in (expected_cot, value_next, transition)))
     discount_factor = discount_of(section)
     return (discount_factor * adjoint_sum, discount_factor * gradient_sum)
 

time: 117 us -> 106 us (0.906)
  Pallas kernels: 107 us -> 99.7 us
  local copies, waits for them, and re-layouts: 4.03 us -> 0 us
    pallas_call x1, Pallas kernels: 107 us -> 99.7 us  [exchanged(): pl.pallas_call(functools.partial(kernel, n_z), out_shape=(jax.ShapeDtypeS...]
    unnamed x6 -> x0, local copies, waits for them, and re-layouts: 4.03 us -> none
where the time goes in v3:
time: 106 us; the launch traced here: 105 us
  Pallas kernels  99.7 us (94%)
  other arithmetic  4.39 us (4%)
  between operations  1.33 us (1%)
    pallas_call x1, Pallas kernels, exchanged(): pl.pallas_call(functools.partial(kernel, n_z), out_shape=(jax.ShapeDtypeS...  99.7 us
    mul x2, other arithmetic, exchanged(): return (discount_factor * adjoint_sum, discount_factor * gradient_sum)  4.39 us

profile of v3, /device:TPU:1, one launch (start us, length us, event | category | flops | bytes accessed | tf_op | source)
XLA Modules:
  0.0 105.4 jit_solution(14891821274690824983)
XLA Ops:
  1.3 99.7 %shard_map.59 = (f32[1024,512]{1,0:T(8,128)S(1)}, f32[1024,1024]{1,0:T(8,128)S(1)}) custom-call(bf16[1024,512]{1,0:T(8,128)(2,1)} %c_in.1, bf16[1024,512]{1,0:T(8,128)(2,1)} %v_in.1, bf16[1024,1024]{1,0:T(8,128)(2,1)} %t_in.1), custom_call_target="tpu_custom_call" | custom-call | tf_op jit(solution)/shard_map/pallas_call | solution.py:369
  101.0 1.5 %broadcast_multiply_fusion.1 = f32[1024,512]{1,0:T(8,128)} fusion(f32[1024,512]{1,0:T(8,128)S(1)} %get-tuple-element.4, f32[]{:T(128)} %bitcast), kind=kLoop, calls=%fused_computation.1 | loop fusion | flops 524288 | bytes 4194308 | tf_op jit(solution)/shard_map/mul | solution.py:396
  102.6 2.8 %broadcast_multiply_fusion = f32[1024,1024]{1,0:T(8,128)} fusion(f32[1024,1024]{1,0:T(8,128)S(1)} %get-tuple-element.5, f32[]{:T(128)} %bitcast), kind=kLoop, calls=%fused_computation | loop fusion | flops 1048576 | bytes 8388612 | tf_op jit(solution)/shard_map/mul | solution.py:396
